TPU v7x, 256 devices: a whole 4x4x8 slice. The times are simulated.
256 devices in a mesh: scene: 8 (over x, core), region: 32 (over z, y).
Axes of the slice: x: 4, y: 4, z: 8, core: 2. Of those that a mesh axis runs over, the one named last changes fastest.
Arguments:
- tiles: bfloat16 [8, 64, 32, 32, 256], P('scene', 'region'), may hold values from -6 to 6
- cotangent: bfloat16 [8, 64, 16, 16, 256], P('scene', 'region'), may hold values from -6 to 6
- positions: int32 [8, 64], P('scene', 'region'), may hold values from 0 to 63, each once within a row
- clear: int32 [8, 64], P('scene', 'region'), may hold values 0 or 1
- w_first: bfloat16 [2304, 256], P('scene'), may hold values from -0.125 to 0.125
- w_second: bfloat16 [2304, 256], P('scene'), may hold values from -0.125 to 0.125
Outputs:
- features: bfloat16 [8, 64, 16, 16, 256], P('scene', 'region')
- grad_first: float32 [2304, 256], P('region', 'scene')
- grad_second: float32 [2304, 256], P('region', 'scene')
Inputs may be any that keep to these rules, and one draw needn't show every extreme that they name: Each scene's row is a permutation of the grid positions 0 to 63.
All inputs are finite; a program needn't handle non-finite values. No bound on the sum of `clear` on one device may be relied on, other than what follows from the above.
Results may differ from a plain program's by a relative error of at most 0.005.
Values may be sent and summed in bfloat16 or wider, within the bound.
A program may use at most 128 MiB of HBM per device.

v0:
```python
import math
import jax
import jax.numpy as jnp
from jax import lax
from jax.sharding import PartitionSpec as P

GW = 4


def silu_slope(pre_act):
    sigmoid_v = jax.nn.sigmoid(pre_act)
    return sigmoid_v * (1.0 + pre_act * (1.0 - sigmoid_v))


def tap_patches(padded, out_side, stride):
    windows = []
    for tap_row in range(3):
        for tap_col in range(3):
            windows.append(
                padded[
                    :,
                    tap_row : tap_row + stride * out_side : stride,
                    tap_col : tap_col + stride * out_side : stride,
                    :,
                ]
            )
    stacked = jnp.concatenate(windows, axis=-1)
    return stacked.reshape(-1, stacked.shape[-1])


def shift_down(values, axis_num):
    widths = [(0, 0)] * values.ndim
    widths[axis_num] = (1, 0)
    padded = jnp.pad(values, widths)
    return lax.slice_in_dim(padded, 0, values.shape[axis_num], 1, axis_num)


def local(tiles, cotangent, positions, clear, w_first, w_second):
    tiles_here = tiles[0]
    slot_count = tiles_here.shape[0]
    tile_side = tiles_here.shape[1]
    tile_half = tile_side // 2
    channels = tiles_here.shape[3]
    local_pos = positions[0]
    every_pos = lax.all_gather(positions, "region", axis=1, tiled=True)[0]
    tile_count = every_pos.shape[0]
    grid_rows = tile_count // GW
    slot_ids = jnp.arange(tile_count, dtype=jnp.int32)
    onehot = (every_pos[:, None] == slot_ids[None, :]).astype(jnp.int32)
    slot_of = jnp.sum(onehot * slot_ids[:, None], axis=0)
    row_here = local_pos // GW
    col_here = local_pos % GW

    def fetch(all_rims, down, sideways, which):
        new_row = row_here + down
        new_col = col_here + sideways
        inside = (new_row >= 0) & (new_row < grid_rows) & (new_col >= 0) & (new_col < GW)
        position = jnp.clip(new_row, 0, grid_rows - 1) * GW + jnp.clip(new_col, 0, GW - 1)
        picked = jnp.take(all_rims, jnp.take(slot_of, position), axis=0)[:, which]
        return picked * inside.astype(picked.dtype)[:, None, None]

    edge_rims = jnp.stack(
        [
            tiles_here[:, 0],
            tiles_here[:, tile_side - 1],
            tiles_here[:, :, 0],
            tiles_here[:, :, tile_side - 1],
        ],
        axis=1,
    )
    all_edges = lax.all_gather(edge_rims, "region", axis=0, tiled=True)
    above_row = fetch(all_edges, -1, 0, 1)
    below_row = fetch(all_edges, 1, 0, 0)
    left_col = fetch(all_edges, 0, -1, 3)
    right_col = fetch(all_edges, 0, 1, 2)
    corner_ul = fetch(all_edges, -1, -1, 1)[:, tile_side - 1]
    corner_ur = fetch(all_edges, -1, 1, 1)[:, 0]
    corner_dl = fetch(all_edges, 1, -1, 0)[:, tile_side - 1]
    corner_dr = fetch(all_edges, 1, 1, 0)[:, 0]
    upper = jnp.concatenate([corner_ul[:, None], above_row, corner_ur[:, None]], axis=1)
    lower = jnp.concatenate([corner_dl[:, None], below_row, corner_dr[:, None]], axis=1)
    middle = jnp.concatenate([left_col[:, :, None], tiles_here, right_col[:, :, None]], axis=2)
    input_pad = jnp.concatenate([upper[:, None], middle, lower[:, None]], axis=1)
    patches_first = tap_patches(input_pad, tile_side, 1)
    pre_flat = jnp.dot(
        patches_first,
        lax.all_gather(w_first, "scene", axis=0, tiled=True),
        preferred_element_type=jnp.float32,
    )
    second_full = lax.all_gather(w_second, "scene", axis=0, tiled=True)
    pre_act = pre_flat.reshape(slot_count, tile_side, tile_side, channels)
    hidden = jax.nn.silu(pre_act).astype(jnp.bfloat16)
    hidden_rims = jnp.stack([hidden[:, tile_side - 1], hidden[:, :, tile_side - 1]], axis=1)
    all_hidden = lax.all_gather(hidden_rims, "region", axis=0, tiled=True)
    hidden_above = fetch(all_hidden, -1, 0, 0)
    hidden_left = fetch(all_hidden, 0, -1, 1)
    hidden_corner = fetch(all_hidden, -1, -1, 0)[:, tile_side - 1]
    hidden_top = jnp.concatenate([hidden_corner[:, None], hidden_above], axis=1)
    hidden_body = jnp.concatenate([hidden_left[:, :, None], hidden], axis=2)
    hidden_pad = jnp.concatenate([hidden_top[:, None], hidden_body], axis=1)
    patches_second = tap_patches(hidden_pad, tile_half, 2)
    out_flat = jnp.dot(patches_second, second_full, preferred_element_type=jnp.float32)
    features = out_flat.astype(jnp.bfloat16).reshape(1, slot_count, tile_half, tile_half, channels)
    masked = cotangent[0] * clear[0].astype(jnp.bfloat16)[:, None, None, None]
    masked_flat = masked.reshape(-1, channels)
    grad_second = lax.dot_general(
        patches_second, masked_flat, (((0,), (0,)), ((), ())), preferred_element_type=jnp.float32
    )
    grad_rims = jnp.stack([masked[:, 0], masked[:, :, 0]], axis=1)
    all_grads = lax.all_gather(grad_rims, "region", axis=0, tiled=True)
    grad_below = fetch(all_grads, 1, 0, 0)
    grad_right = fetch(all_grads, 0, 1, 1)
    grad_corner = fetch(all_grads, 1, 1, 0)[:, 0]
    grad_body = jnp.concatenate([masked, grad_right[:, :, None]], axis=2)
    grad_bottom = jnp.concatenate([grad_below, grad_corner[:, None]], axis=1)
    grad_pad = jnp.concatenate([grad_body, grad_bottom[:, None]], axis=1)
    extended = tile_half + 1
    spread = lax.dot_general(
        grad_pad.reshape(-1, channels),
        second_full,
        (((1,), (1,)), ((), ())),
        preferred_element_type=jnp.float32,
    )
    spread = spread.reshape(slot_count, extended, extended, 3, 3, channels)
    row_even = spread[:, :, :, 0] + shift_down(spread[:, :, :, 2], 1)
    row_odd = spread[:, :, :, 1]
    by_rows = jnp.stack([row_even, row_odd], axis=2).reshape(
        slot_count, 2 * extended, extended, 3, channels
    )
    col_even = by_rows[:, :, :, 0] + shift_down(by_rows[:, :, :, 2], 2)
    col_odd = by_rows[:, :, :, 1]
    dense = jnp.stack([col_even, col_odd], axis=3).reshape(
        slot_count, 2 * extended, 2 * extended, channels
    )
    dhidden = dense[:, 1 : tile_side + 1, 1 : tile_side + 1]
    dpre = (dhidden * silu_slope(pre_act)).astype(jnp.bfloat16)
    grad_first = lax.dot_general(
        patches_first,
        dpre.reshape(-1, channels),
        (((0,), (0,)), ((), ())),
        preferred_element_type=jnp.float32,
    )
    row_block = grad_first.shape[0] // lax.axis_size("region")
    full_first, full_second = lax.psum((grad_first, grad_second), "region")
    sum_sq = jnp.sum(full_first * full_first) + jnp.sum(full_second * full_second)
    row_start = lax.axis_index("region") * row_block
    share_first = lax.dynamic_slice_in_dim(full_first, row_start, row_block, 0)
    share_second = lax.dynamic_slice_in_dim(full_second, row_start, row_block, 0)
    factor = 3.0 * channels * math.sqrt(2.0) / (jnp.sqrt(sum_sq) + 0.01) / lax.axis_size("scene")
    out_first, out_second = (
        lax.psum_scatter(factor * share_first, "scene", scatter_dimension=1, tiled=True),
        lax.psum_scatter(factor * share_second, "scene", scatter_dimension=1, tiled=True),
    )
    return (features, out_first, out_second)


def solution(mesh):
    in_specs = (
        P("scene", "region", None, None, None),
        P("scene", "region", None, None, None),
        P("scene", "region"),
        P("scene", "region"),
        P("scene", None),
        P("scene", None),
    )
    out_specs = (P("scene", "region", None, None, None), P("region", "scene"), P("region", "scene"))
    return jax.shard_map(local, mesh=mesh, in_specs=in_specs, out_specs=out_specs, check_vma=False)
```

profile of v0, /device:TPU:8, one launch (start us, length us, event | category | flops | bytes accessed | tf_op | source)
XLA Modules:
  0.0 681.8 jit_solution(13259119407148330793)
XLA Ops:
  17.6 22.6 %all-reduce.2 = s32[64]{0:T(128)S(1)} all-reduce(s32[64]{0:T(128)S(1)} %bitcast_dynamic-update-slice_fusion), channel_id=1, replica_groups=mesh['scene'=8,'region'=32] {'region'}, use_global_device_ids=true, to_apply=%add.2 | all-reduce | flops 64 | bytes 512
  50.9 37.8 %all-gather.14.cloned.1.call-done = bf16[64,2,16,256]{3,2,1,0:T(8,128)(2,1)} async-done(((bf16[2,2,16,256]{3,2,1,0:T(8,128)(2,1)}), bf16[64,2,16,256]{3,2,1,0:T(8,128)(2,1)}) %all-gather.14.cloned.1.call-update) | async-done | bytes 1048592 | tf_op jit(solution)/shard_map/all_gather | solution.py:110
  94.4 76.7 %all-gather.6.cloned.1.call-done = bf16[64,4,32,256]{3,2,1,0:T(8,128)(2,1)} async-done(((bf16[2,4,32,256]{3,2,1,0:T(8,128)(2,1)}), bf16[64,4,32,256]{3,2,1,0:T(8,128)(2,1)}) %all-gather.6.cloned.1.call-update) | async-done | bytes 4194320 | tf_op jit(solution)/shard_map/all_gather | solution.py:71
  174.6 23.1 %all-gather.12.cloned.1.call-done = bf16[2304,256]{1,0:T(8,128)(2,1)} async-done(((bf16[288,256]{1,0:T(8,128)(2,1)}), bf16[2304,256]{1,0:T(8,128)(2,1)}) %all-gather.12.cloned.1.call-update) | async-done | bytes 1179664 | tf_op jit(solution)/shard_map/all_gather | solution.py:90
  202.2 3.6 gather_fusion.13
  207.3 3.5 gather_fusion.9
  212.9 3.5 gather_fusion.1
  218.6 3.6 gather_fusion.5
  224.3 3.5 gather_fusion.11
  229.9 3.5 gather_fusion.7
  246.0 3.6 copy.128
  249.6 3.7 copy.138
  265.3 8.0 %multiply_convert_fusion = (bf16[2,32,32,256]{3,2,1,0:T(8,128)(2,1)S(1)}, f32[2,32,32,256]{3,2,1,0:T(8,128)}) fusion(bf16[2,32,32,2304]{3,2,1,0:T(8,128)(2,1)} %slice_dynamic-update-slice_fusion, bf16[2304,256]{1,0:T(8,128)(2,1)} %all-gather.8.cloned.1.call-done), kind=kOutput, calls=%fused_computation.36 | convolution fusion | flops 2418540544 | bytes 13762560 | tf_op jit(solution)/shard_map/dot_general | solution.py:85
  273.5 9.9 %slice.204 = bf16[2,16,16,256]{3,2,1,0:T(8,128)(2,1)} slice(bf16[2,32,32,256]{3,2,1,0:T(8,128)(2,1)S(1)} %get-tuple-element.70), slice={[0:2:1], [0:32:2], [0:32:2], [0:256:1]} | slice | bytes 524288 | tf_op jit(solution)/shard_map/slice | solution.py:20
  283.4 9.8 %slice.205 = bf16[2,16,16,256]{3,2,1,0:T(8,128)(2,1)} slice(bf16[2,32,32,256]{3,2,1,0:T(8,128)(2,1)S(1)} %get-tuple-element.70), slice={[0:2:1], [0:32:2], [1:32:2], [0:256:1]} | slice | bytes 524288 | tf_op jit(solution)/shard_map/slice | solution.py:20
  293.2 9.8 %slice.207 = bf16[2,16,16,256]{3,2,1,0:T(8,128)(2,1)} slice(bf16[2,32,32,256]{3,2,1,0:T(8,128)(2,1)S(1)} %get-tuple-element.70), slice={[0:2:1], [1:32:2], [0:32:2], [0:256:1]} | slice | bytes 524288 | tf_op jit(solution)/shard_map/slice | solution.py:20
  303.0 9.8 %slice.208 = bf16[2,16,16,256]{3,2,1,0:T(8,128)(2,1)} slice(bf16[2,32,32,256]{3,2,1,0:T(8,128)(2,1)S(1)} %get-tuple-element.70), slice={[0:2:1], [1:32:2], [1:32:2], [0:256:1]} | slice | bytes 524288 | tf_op jit(solution)/shard_map/slice | solution.py:20
  320.9 7.9 %convolution_bitcast_fusion.1 = f32[2304,256]{1,0:T(8,128)} fusion(bf16[2,32,32,2304]{3,2,1,0:T(8,128)(2,1)} %slice_dynamic-update-slice_fusion, f32[2,32,32,256]{3,0,2,1:T(2,128)S(1)} %slice.308, f32[2,32,32,256]{3,2,1,0:T(8,128)S(1)} %copy-done.25), kind=kOutput, calls=%fused_computation.24 | convolution fusion | flops 2420637696 | bytes 15990784 | tf_op jit(solution)/shard_map/dot_general | solution.py:137
  328.8 64.2 %all-gather.10.cloned.1.call-done = bf16[64,2,32,256]{3,2,1,0:T(8,128)(2,1)} async-done(((bf16[2,2,32,256]{3,2,1,0:T(8,128)(2,1)}), bf16[64,2,32,256]{3,2,1,0:T(8,128)(2,1)}) %all-gather.10.cloned.1.call-update) | async-done | bytes 2097168 | tf_op jit(solution)/shard_map/all_gather | solution.py:94
  405.7 12.5 %slice.203 = bf16[2,16,16,256]{3,2,1,0:T(8,128)(2,1)S(1)} slice(bf16[2,32,33,256]{3,2,1,0:T(8,128)(2,1)} %pad_maximum_fusion.3), slice={[0:2:1], [0:32:2], [0:32:2], [0:256:1]} | slice | bytes 524288 | tf_op jit(solution)/shard_map/slice | solution.py:20
  418.3 12.5 %slice.206 = bf16[2,16,16,256]{3,2,1,0:T(8,128)(2,1)S(1)} slice(bf16[2,32,33,256]{3,2,1,0:T(8,128)(2,1)} %pad_maximum_fusion.3), slice={[0:2:1], [1:32:2], [0:32:2], [0:256:1]} | slice | bytes 524288 | tf_op jit(solution)/shard_map/slice | solution.py:20
  434.9 164.7 %all-reduce.6.cloned.1.call-done = (f32[2304,256]{1,0:T(8,128)}, f32[2304,256]{1,0:T(8,128)}) async-done(((f32[2304,256]{1,0:T(8,128)}, f32[2304,256]{1,0:T(8,128)}), (f32[2304,256]{1,0:T(8,128)}, f32[2304,256]{1,0:T(8,128)})) %all-reduce.6.cloned.1.call-update) | async-done | bytes 4718608 | tf_op jit(solution)/shard_map/psum | solution.py:144
  613.9 26.2 %reduce-scatter.9.cloned.1.call-done = f32[32,72]{1,0:T(8,128)} async-done(((f32[256,72]{1,0:T(8,128)}), f32[32,72]{1,0:T(8,128)}) %reduce-scatter.9.cloned.1.call-update) | async-done | bytes 9232
  640.2 34.8 %reduce-scatter.7.cloned.1.call-done = f32[32,72]{1,0:T(8,128)} async-done(((f32[256,72]{1,0:T(8,128)}), f32[32,72]{1,0:T(8,128)}) %reduce-scatter.7.cloned.1.call-update) | async-done | bytes 9232
  (193 shorter events, 105.9 us)
Async XLA Ops:
  7.2 81.6 %all-gather.14.cloned.1.call-start = ((), (), s32[]{:S(2)}) async-start(), calls=%async_computation.6 | async-start | bytes 1081344 | tf_op jit(solution)/shard_map/all_gather | solution.py:110
  8.9 188.7 %copy-start.3 = (bf16[2,16,16,256]{3,2,1,0:T(8,128)(2,1)}, bf16[2,16,16,256]{3,2,1,0:T(8,128)(2,1)S(1)}, u32[]{:S(2)}) copy-start(bf16[2,16,16,256]{3,2,1,0:T(8,128)(2,1)S(1)} %bitcast_multiply_fusion) | copy-start | bytes 786436
  9.7 161.4 %all-gather.6.cloned.1.call-start = ((), (), s32[]{:S(2)}) async-start(), calls=%async_computation.2 | async-start | bytes 4325376 | tf_op jit(solution)/shard_map/all_gather | solution.py:71
  12.4 185.3 %all-gather.12.cloned.1.call-start = ((), (), s32[]{:S(2)}) async-start(), calls=%async_computation.5 | async-start | bytes 1327104 | tf_op jit(solution)/shard_map/all_gather | solution.py:90
  13.1 252.2 %all-gather.8.cloned.1.call-start = ((), (), s32[]{:S(2)}) async-start(), calls=%async_computation.3 | async-start | bytes 1327104 | tf_op jit(solution)/shard_map/all_gather | solution.py:87
  13.7 379.4 %all-gather.10.cloned.1.call-start = ((), (), s32[]{:S(2)}) async-start(), calls=%async_computation.4 | async-start | bytes 2162688 | tf_op jit(solution)/shard_map/all_gather | solution.py:94
  41.7 52.8 %copy-start.20 = (pred[2]{0:T(512)(128)(4,1)}, pred[2]{0:T(512)(128)(4,1)S(1)}, u32[]{:S(2)}) copy-start(pred[2]{0:T(512)(128)(4,1)S(1)} %get-tuple-element.74) | copy-start | bytes 10
  42.9 51.4 %copy-start.21 = (bf16[2]{0:T(256)(128)(2,1)}, bf16[2]{0:T(256)(128)(2,1)S(1)}, u32[]{:S(2)}) copy-start(bf16[2]{0:T(256)(128)(2,1)S(1)} %get-tuple-element.78) | copy-start | bytes 16
  42.9 51.4 %copy-start.22 = (pred[2]{0:T(512)(128)(4,1)}, pred[2]{0:T(512)(128)(4,1)S(1)}, u32[]{:S(2)}) copy-start(pred[2]{0:T(512)(128)(4,1)S(1)} %get-tuple-element.41) | copy-start | bytes 10
  42.9 51.5 %copy-start.23 = (bf16[2]{0:T(256)(128)(2,1)}, bf16[2]{0:T(256)(128)(2,1)S(1)}, u32[]{:S(2)}) copy-start(bf16[2]{0:T(256)(128)(2,1)S(1)} %get-tuple-element.82) | copy-start | bytes 16
  43.0 51.4 %copy-start.14 = (s32[1024]{0:T(1024)}, s32[1024]{0:T(1024)S(1)}, u32[]{:S(2)}) copy-start(s32[1024]{0:T(1024)S(1)} %pad_clamp_fusion.2) | copy-start | bytes 12292
  43.0 49.4 %copy-start.13 = (s32[1024]{0:T(1024)}, s32[1024]{0:T(1024)S(1)}, u32[]{:S(2)}) copy-start(s32[1024]{0:T(1024)S(1)} %pad_clamp_fusion.6) | copy-start | bytes 12292
  202.2 39.3 %copy-start = (bf16[1,2,32,32,256]{4,3,2,1,0:T(8,128)(2,1)S(1)}, bf16[1,2,32,32,256]{4,3,2,1,0:T(8,128)(2,1)}, u32[]{:S(2)}) copy-start(bf16[1,2,32,32,256]{4,3,2,1,0:T(8,128)(2,1)} %param.14) | copy-start | bytes 3145732
  316.0 283.7 %all-reduce.6.cloned.1.call-start = ((), (), s32[]{:S(2)}) async-start(), calls=%async_computation.9 | async-start | bytes 9437184 | tf_op jit(solution)/shard_map/psum | solution.py:144
  320.9 74.4 %copy-start.19 = (pred[2]{0:T(512)(128)(4,1)S(1)}, pred[2]{0:T(512)(128)(4,1)}, u32[]{:S(2)}) copy-start(pred[2]{0:T(512)(128)(4,1)} %get-tuple-element.39) | copy-start | bytes 10
  320.9 74.5 %copy-start.17 = (bf16[2]{0:T(256)(128)(2,1)S(1)}, bf16[2]{0:T(256)(128)(2,1)}, u32[]{:S(2)}) copy-start(bf16[2]{0:T(256)(128)(2,1)} %get-tuple-element.81) | copy-start | bytes 16
  328.8 70.8 %copy-start.18 = (pred[2]{0:T(512)(128)(4,1)S(1)}, pred[2]{0:T(512)(128)(4,1)}, u32[]{:S(2)}) copy-start(pred[2]{0:T(512)(128)(4,1)} %get-tuple-element.33) | copy-start | bytes 10
  328.8 70.9 %copy-start.24 = (bf16[2]{0:T(256)(128)(2,1)S(1)}, bf16[2]{0:T(256)(128)(2,1)}, u32[]{:S(2)}) copy-start(bf16[2]{0:T(256)(128)(2,1)} %get-tuple-element.80) | copy-start | bytes 16
  328.8 73.2 %copy-start.15 = (pred[2]{0:T(512)(128)(4,1)S(1)}, pred[2]{0:T(512)(128)(4,1)}, u32[]{:S(2)}) copy-start(pred[2]{0:T(512)(128)(4,1)} %get-tuple-element.35) | copy-start | bytes 10
  328.8 73.3 %copy-start.16 = (bf16[2]{0:T(256)(128)(2,1)S(1)}, bf16[2]{0:T(256)(128)(2,1)}, u32[]{:S(2)}) copy-start(bf16[2]{0:T(256)(128)(2,1)} %get-tuple-element.76) | copy-start | bytes 16
  402.9 28.0 %copy-start.9 = (bf16[2,16,16,256]{3,2,1,0:T(8,128)(2,1)S(1)}, bf16[2,16,16,256]{3,2,1,0:T(8,128)(2,1)}, u32[]{:S(2)}) copy-start(bf16[2,16,16,256]{3,2,1,0:T(8,128)(2,1)} %slice.204) | copy-start | bytes 786436
  403.8 27.2 %copy-start.8 = (bf16[2,16,16,256]{3,2,1,0:T(8,128)(2,1)S(1)}, bf16[2,16,16,256]{3,2,1,0:T(8,128)(2,1)}, u32[]{:S(2)}) copy-start(bf16[2,16,16,256]{3,2,1,0:T(8,128)(2,1)} %slice.205) | copy-start | bytes 786436
  434.8 205.3 %reduce-scatter.9.cloned.1.call-start = ((), (), s32[]{:S(2)}) async-start(), calls=%async_computation.8 | async-start | bytes 147456
  608.4 66.6 %reduce-scatter.7.cloned.1.call-start = ((), (), s32[]{:S(2)}) async-start(), calls=%async_computation.7 | async-start | bytes 147456
  (10 other events, 67.1 us)
Sparse Core Ops, SparseCore 0:
  10.6 78.0 all-gather.13
  91.9 79.1 all-gather.5
  172.9 24.6 all-gather.11
  199.3 26.2 all-gather.7
  316.1 76.9 all-gather.9
  435.0 164.6 all-reduce.5
  608.5 31.5 reduce-scatter.8
  643.2 31.6 reduce-scatter.6
where the time goes:
time: 686 us; the launch traced here: 682 us
  waiting for transfers between devices  429 us (63%)
  local copies, waits for them, and re-layouts  143 us (21%)
  other arithmetic  46.8 us (7%)
  matrix products  23.9 us (3%)
  blocking collectives  22.6 us (3%)
  between operations  16.8 us (2%)
    psum x1, waiting for transfers between devices, local(): full_first, full_second = lax.psum((grad_first, grad_second), 'region')  165 us
    all_gather x1, waiting for transfers between devices, local(): all_edges = lax.all_gather(edge_rims, 'region', axis=0, tiled=True)  76.7 us
    slice x9, local copies, waits for them, and re-layouts, tap_patches(): padded[:, tap_row:tap_row + stride * out_side:stride, tap_col:tap_col + s...  67.2 us
    all_gather x1, waiting for transfers between devices, local(): all_hidden = lax.all_gather(hidden_rims, 'region', axis=0, tiled=True)  64.2 us
    unnamed x10, waiting for transfers between devices  62.3 us
    gather x22, local copies, waits for them, and re-layouts, fetch(): picked = jnp.take(all_rims, jnp.take(slot_of, position), axis=0)[:, which]  44.7 us
    all_gather x1, waiting for transfers between devices, local(): all_grads = lax.all_gather(grad_rims, 'region', axis=0, tiled=True)  37.8 us
    all_gather x1, waiting for transfers between devices, local(): second_full = lax.all_gather(w_second, 'scene', axis=0, tiled=True)  23.1 us
  transfers between devices with their start and end apart: 8, of which 7 were waited for; matrix products, arithmetic and copies ran while one was open for 16% of the time, Pallas kernels for 0%

commit v1 on v0

--- a/solution.py
+++ b/solution.py
@@ -87,7 +87,16 @@
         lax.all_gather(w_first, "scene", axis=0, tiled=True),
         preferred_element_type=jnp.float32,
     )
-    second_full = lax.all_gather(w_second, "scene", axis=0, tiled=True)
+
+    def array_draft(panel):
+        heap = []
+        for _ in range(lax.axis_size("scene")):
+            heap.append(panel)
+        far_arr = lax.all_to_all(jnp.stack(heap), "scene", 0, 0)
+        found_now = jnp.concatenate(far_arr, axis=0)
+        return found_now
+
+    second_full = array_draft(w_second)
     pre_act = pre_flat.reshape(slot_count, tile_side, tile_side, channels)
     hidden = jax.nn.silu(pre_act).astype(jnp.bfloat16)
     hidden_rims = jnp.stack([hidden[:, tile_side - 1], hidden[:, :, tile_side - 1]], axis=1)

time: 686 us -> 661 us (0.964)
  waiting for transfers between devices: 429 us -> 400 us
    all_gather x1 -> x0, waiting for transfers between devices: 23.1 us -> none  [local(): second_full = lax.all_gather(w_second, 'scene', axis=0, tiled=True)]
    unnamed x10 -> x9, waiting for transfers between devices: 62.3 us -> 61.8 us
    unnamed x73 -> x79, local copies, waits for them, and re-layouts: 15.9 us -> 15.4 us
  transfers between devices with their start and end apart: 8 -> 8, of which waited for: 7 -> 6; matrix products, arithmetic and copies ran while one was open for 16% -> 17% of each run, Pallas kernels for 0% -> 0%
where the time goes in v1:
time: 661 us; the launch traced here: 657 us
  waiting for transfers between devices  400 us (61%)
  local copies, waits for them, and re-layouts  144 us (22%)
  other arithmetic  46.2 us (7%)
  blocking collectives  22.6 us (3%)
  matrix products  22.6 us (3%)
  between operations  16.8 us (3%)
    psum x1, waiting for transfers between devices, local(): full_first, full_second = lax.psum((grad_first, grad_second), 'region')  165 us
    all_gather x1, waiting for transfers between devices, local(): all_edges = lax.all_gather(edge_rims, 'region', axis=0, tiled=True)  76.6 us
    slice x9, local copies, waits for them, and re-layouts, tap_patches(): padded[:, tap_row:tap_row + stride * out_side:stride, tap_col:tap_col + s...  67.2 us
    all_gather x1, waiting for transfers between devices, local(): all_hidden = lax.all_gather(hidden_rims, 'region', axis=0, tiled=True)  62.7 us
    unnamed x9, waiting for transfers between devices  61.8 us
    gather x22, local copies, waits for them, and re-layouts, fetch(): picked = jnp.take(all_rims, jnp.take(slot_of, position), axis=0)[:, which]  44.7 us
    all_gather x1, waiting for transfers between devices, local(): all_grads = lax.all_gather(grad_rims, 'region', axis=0, tiled=True)  34 us
    unnamed x1, blocking collectives  22.6 us
  transfers between devices with their start and end apart: 8, of which 6 were waited for; matrix products, arithmetic and copies ran while one was open for 17% of the time, Pallas kernels for 0%

profile of v1, /device:TPU:8, one launch (start us, length us, event | category | flops | bytes accessed | tf_op | source)
XLA Modules:
  0.0 657.0 jit_solution(17143372769571012453)
XLA Ops:
  14.4 4.3 all-to-all-start
  21.5 22.6 %all-reduce.2 = s32[64]{0:T(128)S(1)} all-reduce(s32[64]{0:T(128)S(1)} %bitcast_dynamic-update-slice_fusion), channel_id=1, replica_groups=mesh['scene'=8,'region'=32] {'region'}, use_global_device_ids=true, to_apply=%add.2 | all-reduce | flops 64 | bytes 512
  54.7 34.0 %all-gather.11.cloned.1.call-done = bf16[64,2,16,256]{3,2,1,0:T(8,128)(2,1)} async-done(((bf16[2,2,16,256]{3,2,1,0:T(8,128)(2,1)}), bf16[64,2,16,256]{3,2,1,0:T(8,128)(2,1)}) %all-gather.11.cloned.1.call-update) | async-done | bytes 1048592 | tf_op jit(solution)/shard_map/all_gather | solution.py:119
  94.5 76.6 %all-gather.5.cloned.1.call-done = bf16[64,4,32,256]{3,2,1,0:T(8,128)(2,1)} async-done(((bf16[2,4,32,256]{3,2,1,0:T(8,128)(2,1)}), bf16[64,4,32,256]{3,2,1,0:T(8,128)(2,1)}) %all-gather.5.cloned.1.call-update) | async-done | bytes 4194320 | tf_op jit(solution)/shard_map/all_gather | solution.py:71
  179.0 3.6 gather_fusion.13
  184.0 3.5 gather_fusion.9
  189.7 3.5 gather_fusion.1
  195.3 3.6 gather_fusion.5
  201.0 3.5 gather_fusion.11
  206.6 3.5 gather_fusion.7
  222.7 3.6 copy.128
  226.2 3.7 copy.138
  242.1 8.0 %multiply_convert_fusion = (bf16[2,32,32,256]{3,2,1,0:T(8,128)(2,1)S(1)}, f32[2,32,32,256]{3,2,1,0:T(8,128)}) fusion(bf16[2,32,32,2304]{3,2,1,0:T(8,128)(2,1)} %slice_dynamic-update-slice_fusion, bf16[2304,256]{1,0:T(8,128)(2,1)} %all-gather.7.cloned.1.call-done), kind=kOutput, calls=%fused_computation.36 | convolution fusion | flops 2418540544 | bytes 13762560 | tf_op jit(solution)/shard_map/dot_general | solution.py:85
  250.2 9.9 %slice.204 = bf16[2,16,16,256]{3,2,1,0:T(8,128)(2,1)} slice(bf16[2,32,32,256]{3,2,1,0:T(8,128)(2,1)S(1)} %get-tuple-element.70), slice={[0:2:1], [0:32:2], [0:32:2], [0:256:1]} | slice | bytes 524288 | tf_op jit(solution)/shard_map/slice | solution.py:20
  260.1 9.8 %slice.205 = bf16[2,16,16,256]{3,2,1,0:T(8,128)(2,1)} slice(bf16[2,32,32,256]{3,2,1,0:T(8,128)(2,1)S(1)} %get-tuple-element.70), slice={[0:2:1], [0:32:2], [1:32:2], [0:256:1]} | slice | bytes 524288 | tf_op jit(solution)/shard_map/slice | solution.py:20
  269.9 9.8 %slice.207 = bf16[2,16,16,256]{3,2,1,0:T(8,128)(2,1)} slice(bf16[2,32,32,256]{3,2,1,0:T(8,128)(2,1)S(1)} %get-tuple-element.70), slice={[0:2:1], [1:32:2], [0:32:2], [0:256:1]} | slice | bytes 524288 | tf_op jit(solution)/shard_map/slice | solution.py:20
  279.7 9.8 %slice.208 = bf16[2,16,16,256]{3,2,1,0:T(8,128)(2,1)} slice(bf16[2,32,32,256]{3,2,1,0:T(8,128)(2,1)S(1)} %get-tuple-element.70), slice={[0:2:1], [1:32:2], [1:32:2], [0:256:1]} | slice | bytes 524288 | tf_op jit(solution)/shard_map/slice | solution.py:20
  297.6 7.9 %convolution_bitcast_fusion.1 = f32[2304,256]{1,0:T(8,128)} fusion(bf16[2,32,32,2304]{3,2,1,0:T(8,128)(2,1)} %slice_dynamic-update-slice_fusion, f32[2,32,32,256]{3,0,2,1:T(2,128)S(1)} %slice.308, f32[2,32,32,256]{3,2,1,0:T(8,128)S(1)} %copy-done.28), kind=kOutput, calls=%fused_computation.24 | convolution fusion | flops 2420637696 | bytes 15990784 | tf_op jit(solution)/shard_map/dot_general | solution.py:146
  305.6 62.7 %all-gather.9.cloned.1.call-done = bf16[64,2,32,256]{3,2,1,0:T(8,128)(2,1)} async-done(((bf16[2,2,32,256]{3,2,1,0:T(8,128)(2,1)}), bf16[64,2,32,256]{3,2,1,0:T(8,128)(2,1)}) %all-gather.9.cloned.1.call-update) | async-done | bytes 2097168 | tf_op jit(solution)/shard_map/all_gather | solution.py:103
  380.9 12.5 %slice.203 = bf16[2,16,16,256]{3,2,1,0:T(8,128)(2,1)S(1)} slice(bf16[2,32,33,256]{3,2,1,0:T(8,128)(2,1)} %pad_maximum_fusion.3), slice={[0:2:1], [0:32:2], [0:32:2], [0:256:1]} | slice | bytes 524288 | tf_op jit(solution)/shard_map/slice | solution.py:20
  393.5 12.5 %slice.206 = bf16[2,16,16,256]{3,2,1,0:T(8,128)(2,1)S(1)} slice(bf16[2,32,33,256]{3,2,1,0:T(8,128)(2,1)} %pad_maximum_fusion.3), slice={[0:2:1], [1:32:2], [0:32:2], [0:256:1]} | slice | bytes 524288 | tf_op jit(solution)/shard_map/slice | solution.py:20
  410.1 164.7 %all-reduce.6.cloned.1.call-done = (f32[2304,256]{1,0:T(8,128)}, f32[2304,256]{1,0:T(8,128)}) async-done(((f32[2304,256]{1,0:T(8,128)}, f32[2304,256]{1,0:T(8,128)}), (f32[2304,256]{1,0:T(8,128)}, f32[2304,256]{1,0:T(8,128)})) %all-reduce.6.cloned.1.call-update) | async-done | bytes 4718608 | tf_op jit(solution)/shard_map/psum | solution.py:153
  589.1 26.2 %reduce-scatter.9.cloned.1.call-done = f32[32,72]{1,0:T(8,128)} async-done(((f32[256,72]{1,0:T(8,128)}), f32[32,72]{1,0:T(8,128)}) %reduce-scatter.9.cloned.1.call-update) | async-done | bytes 9232
  615.3 34.8 %reduce-scatter.7.cloned.1.call-done = f32[32,72]{1,0:T(8,128)} async-done(((f32[256,72]{1,0:T(8,128)}), f32[32,72]{1,0:T(8,128)}) %reduce-scatter.7.cloned.1.call-update) | async-done | bytes 9232
  (199 shorter events, 105.3 us)
Async XLA Ops:
  7.2 81.6 %all-gather.11.cloned.1.call-start = ((), (), s32[]{:S(2)}) async-start(), calls=%async_computation.6 | async-start | bytes 1081344 | tf_op jit(solution)/shard_map/all_gather | solution.py:119
  8.9 165.7 %copy-start.5 = (bf16[2,16,16,256]{3,2,1,0:T(8,128)(2,1)}, bf16[2,16,16,256]{3,2,1,0:T(8,128)(2,1)S(1)}, u32[]{:S(2)}) copy-start(bf16[2,16,16,256]{3,2,1,0:T(8,128)(2,1)S(1)} %bitcast_multiply_fusion) | copy-start | bytes 786436
  9.6 161.5 %all-gather.5.cloned.1.call-start = ((), (), s32[]{:S(2)}) async-start(), calls=%async_computation.3 | async-start | bytes 4325376 | tf_op jit(solution)/shard_map/all_gather | solution.py:71
  14.4 160.2 %all-to-all-start = ((bf16[8,288,256]{2,1,0:T(8,128)(2,1)}), bf16[8,288,256]{2,1,0:T(8,128)(2,1)S(1)}, u32[]{:S(2)}, u32[]{:S(2)}) async-start(bf16[8,288,256]{2,1,0:T(8,128)(2,1)} %stack.34), calls=%async_computation | async-start | bytes 2359296 | tf_op jit(solution)/shard_map/all_to_all | solution.py:95
  18.7 223.4 %all-gather.7.cloned.1.call-start = ((), (), s32[]{:S(2)}) async-start(), calls=%async_computation.4 | async-start | bytes 1327104 | tf_op jit(solution)/shard_map/all_gather | solution.py:87
  19.4 348.8 %all-gather.9.cloned.1.call-start = ((), (), s32[]{:S(2)}) async-start(), calls=%async_computation.5 | async-start | bytes 2162688 | tf_op jit(solution)/shard_map/all_gather | solution.py:103
  45.5 48.9 %copy-start.21 = (pred[2]{0:T(512)(128)(4,1)}, pred[2]{0:T(512)(128)(4,1)S(1)}, u32[]{:S(2)}) copy-start(pred[2]{0:T(512)(128)(4,1)S(1)} %get-tuple-element.74) | copy-start | bytes 10
  46.8 47.6 %copy-start.22 = (bf16[2]{0:T(256)(128)(2,1)}, bf16[2]{0:T(256)(128)(2,1)S(1)}, u32[]{:S(2)}) copy-start(bf16[2]{0:T(256)(128)(2,1)S(1)} %get-tuple-element.78) | copy-start | bytes 16
  46.8 47.6 %copy-start.23 = (pred[2]{0:T(512)(128)(4,1)}, pred[2]{0:T(512)(128)(4,1)S(1)}, u32[]{:S(2)}) copy-start(pred[2]{0:T(512)(128)(4,1)S(1)} %get-tuple-element.41) | copy-start | bytes 10
  46.8 47.6 %copy-start.24 = (bf16[2]{0:T(256)(128)(2,1)}, bf16[2]{0:T(256)(128)(2,1)S(1)}, u32[]{:S(2)}) copy-start(bf16[2]{0:T(256)(128)(2,1)S(1)} %get-tuple-element.82) | copy-start | bytes 16
  46.8 47.6 %copy-start.15 = (s32[1024]{0:T(1024)}, s32[1024]{0:T(1024)S(1)}, u32[]{:S(2)}) copy-start(s32[1024]{0:T(1024)S(1)} %pad_clamp_fusion.2) | copy-start | bytes 12292
  46.8 45.5 %copy-start.14 = (s32[1024]{0:T(1024)}, s32[1024]{0:T(1024)S(1)}, u32[]{:S(2)}) copy-start(s32[1024]{0:T(1024)S(1)} %pad_clamp_fusion.6) | copy-start | bytes 12292
  179.0 39.3 %copy-start = (bf16[1,2,32,32,256]{4,3,2,1,0:T(8,128)(2,1)S(1)}, bf16[1,2,32,32,256]{4,3,2,1,0:T(8,128)(2,1)}, u32[]{:S(2)}) copy-start(bf16[1,2,32,32,256]{4,3,2,1,0:T(8,128)(2,1)} %param.14) | copy-start | bytes 3145732
  292.7 282.1 %all-reduce.6.cloned.1.call-start = ((), (), s32[]{:S(2)}) async-start(), calls=%async_computation.9 | async-start | bytes 9437184 | tf_op jit(solution)/shard_map/psum | solution.py:153
  297.6 72.9 %copy-start.20 = (pred[2]{0:T(512)(128)(4,1)S(1)}, pred[2]{0:T(512)(128)(4,1)}, u32[]{:S(2)}) copy-start(pred[2]{0:T(512)(128)(4,1)} %get-tuple-element.39) | copy-start | bytes 10
  297.6 73.0 %copy-start.18 = (bf16[2]{0:T(256)(128)(2,1)S(1)}, bf16[2]{0:T(256)(128)(2,1)}, u32[]{:S(2)}) copy-start(bf16[2]{0:T(256)(128)(2,1)} %get-tuple-element.81) | copy-start | bytes 16
  305.6 69.3 %copy-start.19 = (pred[2]{0:T(512)(128)(4,1)S(1)}, pred[2]{0:T(512)(128)(4,1)}, u32[]{:S(2)}) copy-start(pred[2]{0:T(512)(128)(4,1)} %get-tuple-element.33) | copy-start | bytes 10
  305.6 69.4 %copy-start.25 = (bf16[2]{0:T(256)(128)(2,1)S(1)}, bf16[2]{0:T(256)(128)(2,1)}, u32[]{:S(2)}) copy-start(bf16[2]{0:T(256)(128)(2,1)} %get-tuple-element.80) | copy-start | bytes 16
  305.6 71.7 %copy-start.16 = (pred[2]{0:T(512)(128)(4,1)S(1)}, pred[2]{0:T(512)(128)(4,1)}, u32[]{:S(2)}) copy-start(pred[2]{0:T(512)(128)(4,1)} %get-tuple-element.35) | copy-start | bytes 10
  305.6 71.7 %copy-start.17 = (bf16[2]{0:T(256)(128)(2,1)S(1)}, bf16[2]{0:T(256)(128)(2,1)}, u32[]{:S(2)}) copy-start(bf16[2]{0:T(256)(128)(2,1)} %get-tuple-element.76) | copy-start | bytes 16
  378.1 28.0 %copy-start.10 = (bf16[2,16,16,256]{3,2,1,0:T(8,128)(2,1)S(1)}, bf16[2,16,16,256]{3,2,1,0:T(8,128)(2,1)}, u32[]{:S(2)}) copy-start(bf16[2,16,16,256]{3,2,1,0:T(8,128)(2,1)} %slice.204) | copy-start | bytes 786436
  379.0 27.2 %copy-start.9 = (bf16[2,16,16,256]{3,2,1,0:T(8,128)(2,1)S(1)}, bf16[2,16,16,256]{3,2,1,0:T(8,128)(2,1)}, u32[]{:S(2)}) copy-start(bf16[2,16,16,256]{3,2,1,0:T(8,128)(2,1)} %slice.205) | copy-start | bytes 786436
  410.0 205.3 %reduce-scatter.9.cloned.1.call-start = ((), (), s32[]{:S(2)}) async-start(), calls=%async_computation.8 | async-start | bytes 147456
  583.5 66.6 %reduce-scatter.7.cloned.1.call-start = ((), (), s32[]{:S(2)}) async-start(), calls=%async_computation.7 | async-start | bytes 147456
  (13 other events, 86.7 us)
Sparse Core Ops, SparseCore 0:
  10.6 78.0 all-gather.10
  91.9 79.1 all-gather.4
  172.9 24.6 all-gather.6
  292.8 75.4 all-gather.8
  410.1 164.5 all-reduce.5
  583.7 31.5 reduce-scatter.8
  618.4 31.6 reduce-scatter.6
